TPU v7x, 32 devices: a whole 2x2x4 slice. The times are simulated.
32 devices in a mesh: leaf: 4 (over x, core), chain: 8 (over z, y).
Axes of the slice: x: 2, y: 2, z: 4, core: 2. Of those that a mesh axis runs over, the one named last changes fastest.
Arguments:
- observations: float32 [32, 128], P(('chain', 'leaf')), may hold values from -6 to 6
- observed: int32 [32, 128], P(('chain', 'leaf')), may hold values 0 or 1
- gaps: float32 [32], P(('chain', 'leaf')), may hold values from 0.015625 to 0.09375
- site_cov: float32 [128, 128], replicated, may hold values from -1 to 1, as said below
Outputs:
- filtered_mean: float32 [32, 256], P(('chain', 'leaf'))
- filtered_cov: float32 [32, 256, 256], P(('chain', 'leaf'))
Inputs may be any that keep to these rules, and one draw needn't show every extreme that they name: site_cov is symmetric with unit diagonal and positive definite.
All inputs are finite; a program needn't handle non-finite values. Where the computation divides by a largest or mean magnitude, that divisor is 1e-20 or more. No bound on the sum of `observed` on one device may be relied on, other than what follows from the above.
Results may differ from a plain program's by a relative error of at most 0.0003.
Values sent between devices are 32-bit elements; how exact they have to be, the bound alone decides.
A program may use at most 128 MiB of HBM per device.

v0:
```python
import functools
import math

import jax
import jax.numpy as jnp
from jax import lax
from jax.experimental import pallas as pl
from jax.experimental.pallas import tpu as pltpu
from jax.sharding import PartitionSpec as P

NEWTON = 13
HIGH = lax.Precision.HIGHEST
NOISE_VAR = 0.3
RATE = math.sqrt(3.0)
SERIES = (
    1.0,
    1.0 / 4.0,
    1.0 / 20.0,
    1.0 / 120.0,
    1.0 / 840.0,
    1.0 / 6720.0,
    1.0 / 60480.0,
    1.0 / 604800.0,
)
SMALL = 4e-3
PAD = 8


def gamma_three(twice, square):
    total = jnp.zeros_like(twice) + SERIES[7]
    for coef in SERIES[6::-1]:
        total = total * twice + coef
    return square * twice * twice * twice / 6.0 * total


def exact(left, right):
    return jnp.dot(left, right, precision=HIGH, preferred_element_type=jnp.float32)


def fast(left, right):
    return jnp.dot(left, right, preferred_element_type=jnp.float32)


def split(x):
    high = x.astype(jnp.bfloat16)
    low = (x - high.astype(jnp.float32)).astype(jnp.bfloat16)
    return high, low


def filter_kernel(steps, count, place_ref, data_ref, cov_ref, mean_ref, out_ref,
                  coef, state, pred, left, power):
    sites = cov_ref.shape[0]
    dim = 2 * sites
    f32 = jnp.float32
    rows = lax.broadcasted_iota(jnp.int32, (sites, sites), 0)
    cols = lax.broadcasted_iota(jnp.int32, (sites, sites), 1)
    eye = (rows == cols).astype(f32)

    gap = data_ref[:, 2 * sites:]
    first = lax.broadcasted_iota(jnp.int32, gap.shape, 0) == 0
    reach = RATE * gap
    decay = jnp.where(first, 0.0, jnp.exp(-reach))
    square = decay * decay
    coef[0] = decay * (1.0 + reach)
    coef[1] = decay * reach
    coef[2] = -decay * reach
    coef[3] = decay * (1.0 - reach)
    coef[4] = jnp.where(first, 1.0, gamma_three(2.0 * reach, square))
    coef[5] = 2.0 * reach * reach * square
    coef[6] = 1.0 - square * (1.0 - 2.0 * reach + 2.0 * reach * reach)
    coef[7] = data_ref[:, sites:2 * sites] / NOISE_VAR
    coef[8] = data_ref[:, :sites]
    state[...] = jnp.zeros_like(state)
    start = place_ref[0] * count

    def step(k, _):
        row = pl.ds(k, 1)
        f00, f01, f10, f11 = (coef[i, row, :] for i in range(4))
        q00, q01, q11 = (coef[i, row, :] for i in range(4, 7))
        weight = coef[7, row, :]
        obs = coef[8, row, :]
        cov = cov_ref[...]

        spp, spv = state[:sites, :sites], state[:sites, sites:]
        svp, svv = state[sites:dim, :sites], state[sites:dim, sites:]
        smp, smv = state[dim:, :sites], state[dim:, sites:]
        lpp, lpv = f00 * spp + f01 * svp, f00 * spv + f01 * svv
        lvp, lvv = f10 * spp + f11 * svp, f10 * spv + f11 * svv
        ppp = f00 * lpp + f01 * lpv + q00 * cov
        ppv = f10 * lpp + f11 * lpv + q01 * cov
        pvp = f00 * lvp + f01 * lvv + q01 * cov
        pvv = f10 * lvp + f11 * lvv + q11 * cov
        pmp = f00 * smp + f01 * smv
        pmv = f10 * smp + f11 * smv
        pred[:sites, :sites] = ppp
        pred[:sites, sites:] = ppv
        pred[sites:dim, :sites] = pvp
        pred[sites:dim, sites:] = pvv
        pred[dim:, :sites] = pmp
        pred[dim:, sites:] = pmv

        diag = 1.0 + weight * jnp.sum(ppp * eye, axis=0, keepdims=True)
        scale = weight / diag
        r = (eye - 1.0) * ppp * scale
        y = jnp.concatenate([ppp * scale, pvp * scale, (pmp - obs) * scale], axis=0)
        rh, rl = split(r)
        yh, yl = split(y)
        r2 = fast(rh, rh)
        right = jnp.concatenate(
            [jnp.concatenate([rh, rl], axis=1)] * 2, axis=0)
        both = fast(jnp.concatenate([yh, yl], axis=1), right)
        y = y + (both[:, :sites] + both[:, sites:])
        trace = jnp.sum(r2 * eye)
        r2h = r2.astype(jnp.bfloat16)
        yh = y.astype(jnp.bfloat16)
        ph, pl_ = split(pred[:sites, :])
        u = fast(yh, r2h)
        z = fast(r2h, ph)
        y = y + u
        yh, yl = split(y)
        last = fast(
            jnp.concatenate([yh, yl, yh, u.astype(jnp.bfloat16)], axis=1),
            jnp.concatenate([ph, ph, pl_, z.astype(jnp.bfloat16)], axis=0))
        state[...] = pred[...] - last

        @pl.when(jnp.logical_not(trace < SMALL))
        def _():
            pp = pred[:sites, :sites]
            off = (1.0 - eye) * pp * scale
            reach_off = jnp.max(jnp.sum(jnp.abs(off), axis=0, keepdims=True), axis=1, keepdims=True)
            most = jnp.max(diag, axis=1, keepdims=True)
            low = jnp.maximum(1.0 / most, 1.0 - reach_off)
            omega = 2.0 / (low + 1.0 + reach_off)
            power[...] = (1.0 - omega) * eye - omega * off
            left[:dim, :] = omega * (pred[:dim, :sites] * scale)
            left[dim:, :] = omega * ((pred[dim:, :sites] - obs) * scale)

            def turn(i, _):
                now = power[...]
                left[...] = left[...] + exact(left[...], now)
                power[...] = exact(now, now)
                return 0

            lax.fori_loop(0, NEWTON, turn, 0)
            state[...] = pred[...] - exact(left[...], pred[:sites, :])

        @pl.when(k >= start)
        def _():
            source = lax.broadcasted_iota(jnp.int32, (dim, dim), 0)
            target = lax.broadcasted_iota(jnp.int32, (dim, dim), 1)
            move = (source == (target % 2) * sites + target // 2).astype(f32)
            wide = exact(state[...], move)
            source = lax.broadcasted_iota(jnp.int32, (dim, dim), 1)
            target = lax.broadcasted_iota(jnp.int32, (dim, dim), 0)
            back = (source == (target % 2) * sites + target // 2).astype(f32)
            out_ref[pl.ds(k - start, 1)] = exact(back, wide[:dim])[None]
            mean_ref[pl.ds(k - start, 1)] = wide[dim:dim + 1][None]

        return 0

    lax.fori_loop(0, start + count, step, 0)


def local(observations, observed, gaps, site_cov):
    count, sites = observations.shape
    dim = 2 * sites
    devices = lax.axis_size("leaf") * lax.axis_size("chain")
    place = lax.axis_index("chain") * lax.axis_size("leaf") + lax.axis_index("leaf")
    steps = count * devices
    packed = jnp.concatenate(
        [observations, observed.astype(jnp.float32),
         jnp.broadcast_to(gaps[:, None], (count, sites))], axis=1)
    data = lax.all_gather(packed, ("chain", "leaf"), axis=0, tiled=True)
    vmem = pl.BlockSpec(memory_space=pltpu.VMEM)
    mean, covs = pl.pallas_call(
        functools.partial(filter_kernel, steps, count),
        out_shape=(
            jax.ShapeDtypeStruct((count, 1, dim), jnp.float32),
            jax.ShapeDtypeStruct((count, dim, dim), jnp.float32),
        ),
        in_specs=[pl.BlockSpec(memory_space=pltpu.SMEM), vmem, vmem],
        out_specs=(vmem, vmem),
        scratch_shapes=[
            pltpu.VMEM((9, steps, sites), jnp.float32),
            pltpu.VMEM((dim + PAD, dim), jnp.float32),
            pltpu.VMEM((dim + PAD, dim), jnp.float32),
            pltpu.VMEM((dim + PAD, sites), jnp.float32),
            pltpu.VMEM((sites, sites), jnp.float32),
        ],
        compiler_params=pltpu.CompilerParams(vmem_limit_bytes=32 * 1024 * 1024),
    )(jnp.reshape(place, (1,)).astype(jnp.int32), data, site_cov)
    return mean.reshape(count, dim), covs


def solution(mesh):
    placed = (P(("chain", "leaf"), None), P(("chain", "leaf"), None), P(("chain", "leaf")), P())
    return jax.shard_map(
        local,
        mesh=mesh,
        in_specs=placed,
        out_specs=(P(("chain", "leaf"), None), P(("chain", "leaf"), None, None)),
        check_vma=False,
    )
```

profile of v0, /device:TPU:31, one launch (start us, length us, event | category | flops | bytes accessed | tf_op | source)
XLA Modules:
  0.0 61.2 jit_solution(7033787486545831097)
XLA Ops:
  1.3 0.0 copy-start.2
  1.3 0.6 %copy-done.2 = s32[1,128]{1,0:T(1,128)S(1)} copy-done((s32[1,128]{1,0:T(1,128)S(1)}, s32[1,128]{1,0:T(1,128)}, u32[]{:S(2)}) %copy-start.2) | copy-done | bytes 536
  1.9 0.0 copy-start.1
  1.9 0.6 %copy-done.1 = f32[1,128]{1,0:T(1,128)S(1)} copy-done((f32[1,128]{1,0:T(1,128)S(1)}, f32[1,128]{1,0:T(1,128)}, u32[]{:S(2)}) %copy-start.1) | copy-done | bytes 536
  2.6 0.0 copy-start
  2.6 36.3 %all-gather = f32[32,1,384]{2,1,0:T(1,128)S(1)} all-gather(f32[1,1,384]{2,1,0:T(1,128)S(1)} %fusion), channel_id=1, replica_groups=mesh['leaf'=4,'chain'=8] {'chain','leaf'}, dimensions={0}, use_global_device_ids=true | all-gather | bytes 50688 | tf_op jit(solution)/shard_map/all_gather | solution.py:173
  38.9 0.0 copy-done
  38.9 22.3 %shard_map.59 = (f32[1,1,256]{2,1,0:T(1,128)}, f32[1,256,256]{2,1,0:T(8,128)}) custom-call(s32[1]{0:T(128)} %bitcast.place_ref, f32[32,384]{1,0:T(8,128)S(1)} %bitcast.9, f32[128,128]{1,0:T(8,128)S(1)} %copy-done), custom_call_target="tpu_custom_call" | custom-call | tf_op jit(solution)/shard_map/pallas_call | solution.py:175
  (5 shorter events, 0.0 us)
Async XLA Ops:
  1.3 0.7 %copy-start.2 = (s32[1,128]{1,0:T(1,128)S(1)}, s32[1,128]{1,0:T(1,128)}, u32[]{:S(2)}) copy-start(s32[1,128]{1,0:T(1,128)} %param.5) | copy-start | bytes 1540
  1.9 0.7 %copy-start.1 = (f32[1,128]{1,0:T(1,128)S(1)}, f32[1,128]{1,0:T(1,128)}, u32[]{:S(2)}) copy-start(f32[1,128]{1,0:T(1,128)} %param.4) | copy-start | bytes 1540
  2.6 36.3 %copy-start = (f32[128,128]{1,0:T(8,128)S(1)}, f32[128,128]{1,0:T(8,128)}, u32[]{:S(2)}) copy-start(f32[128,128]{1,0:T(8,128)} %cov_ref.1) | copy-start | bytes 196612
where the time goes:
time: 61.4 us; the launch traced here: 61.2 us
  blocking collectives  36.3 us (59%)
  Pallas kernels  22.3 us (36%)
  local copies, waits for them, and re-layouts  1.3 us (2%)
  between operations  1.3 us (2%)
    all_gather x1, blocking collectives, local(): data = lax.all_gather(packed, ('chain', 'leaf'), axis=0, tiled=True)  36.3 us
    pallas_call x1, Pallas kernels, local(): pl.pallas_call(functools.partial(filter_kernel, steps, count), out_shape=...  22.3 us
    unnamed x7, local copies, waits for them, and re-layouts  1.29 us

commit v1 on v0

--- a/solution.py
+++ b/solution.py
@@ -56,7 +56,10 @@
     cols = lax.broadcasted_iota(jnp.int32, (sites, sites), 1)
     eye = (rows == cols).astype(f32)
 
-    gap = data_ref[:, 2 * sites:]
+    for k in range(steps):
+        for part, plane in ((0, 8), (1, 7), (2, 0)):
+            coef[plane, pl.ds(k, 1), :] = data_ref[k // count, pl.ds(k % count, 1), pl.ds(part * sites, sites)]
+    gap = coef[0]
     first = lax.broadcasted_iota(jnp.int32, gap.shape, 0) == 0
     reach = RATE * gap
     decay = jnp.where(first, 0.0, jnp.exp(-reach))
@@ -68,8 +71,7 @@
     coef[4] = jnp.where(first, 1.0, gamma_three(2.0 * reach, square))
     coef[5] = 2.0 * reach * reach * square
     coef[6] = 1.0 - square * (1.0 - 2.0 * reach + 2.0 * reach * reach)
-    coef[7] = data_ref[:, sites:2 * sites] / NOISE_VAR
-    coef[8] = data_ref[:, :sites]
+    coef[7] = coef[7] / NOISE_VAR
     state[...] = jnp.zeros_like(state)
     start = place_ref[0] * count
 
@@ -161,6 +163,68 @@
     lax.fori_loop(0, start + count, step, 0)
 
 
+def gather_kernel(chains, leaves, mine_ref, all_ref, own_sem, leaf_send, leaf_recv, chain_send, chain_recv):
+    leaf = lax.axis_index("leaf")
+    chain = lax.axis_index("chain")
+    barrier = pltpu.get_barrier_semaphore()
+    for turn in range(1, chains):
+        there = lax.rem(chain + turn, chains)
+        pl.semaphore_signal(barrier, inc=1, device_id={"chain": there}, device_id_type=pl.DeviceIdType.MESH)
+    for turn in range(1, leaves):
+        there = lax.rem(leaf + turn, leaves)
+        pl.semaphore_signal(barrier, inc=1, device_id={"leaf": there}, device_id_type=pl.DeviceIdType.MESH)
+    own = pltpu.make_async_copy(mine_ref, all_ref.at[chain, leaf], own_sem)
+    own.start()
+    pl.semaphore_wait(barrier, chains + leaves - 2)
+
+    sends = []
+    for turn in range(1, leaves):
+        copy = pltpu.make_async_remote_copy(
+            src_ref=mine_ref,
+            dst_ref=all_ref.at[chain, leaf],
+            send_sem=leaf_send.at[turn - 1],
+            recv_sem=leaf_recv.at[turn - 1],
+            device_id={"leaf": lax.rem(leaf + turn, leaves)},
+            device_id_type=pl.DeviceIdType.MESH,
+        )
+        copy.start()
+        sends.append(copy)
+    own.wait()
+    for copy in sends:
+        copy.wait_recv()
+    later = []
+    for turn in range(chains - 1, 0, -1):
+        copy = pltpu.make_async_remote_copy(
+            src_ref=all_ref.at[chain],
+            dst_ref=all_ref.at[chain],
+            send_sem=chain_send.at[turn - 1],
+            recv_sem=chain_recv.at[turn - 1],
+            device_id={"chain": lax.rem(chain + turn, chains)},
+            device_id_type=pl.DeviceIdType.MESH,
+        )
+        copy.start()
+        later.append(copy)
+    for copy in later:
+        copy.wait_recv()
+    for copy in sends + later:
+        copy.wait_send()
+
+
+def gathered(packed):
+    leaves = lax.axis_size("leaf")
+    chains = lax.axis_size("chain")
+    vmem = pl.BlockSpec(memory_space=pltpu.VMEM)
+    dma = pltpu.SemaphoreType.DMA
+    return pl.pallas_call(
+        functools.partial(gather_kernel, chains, leaves),
+        out_shape=jax.ShapeDtypeStruct((chains, leaves) + packed.shape, packed.dtype),
+        in_specs=[vmem],
+        out_specs=vmem,
+        scratch_shapes=[dma, dma((leaves - 1,)), dma((leaves - 1,)), dma((chains - 1,)), dma((chains - 1,))],
+        compiler_params=pltpu.CompilerParams(collective_id=0, has_side_effects=True),
+    )(packed)
+
+
 def local(observations, observed, gaps, site_cov):
     count, sites = observations.shape
     dim = 2 * sites
@@ -170,7 +234,7 @@
     packed = jnp.concatenate(
         [observations, observed.astype(jnp.float32),
          jnp.broadcast_to(gaps[:, None], (count, sites))], axis=1)
-    data = lax.all_gather(packed, ("chain", "leaf"), axis=0, tiled=True)
+    data = gathered(packed).reshape(devices, count, 3 * sites)
     vmem = pl.BlockSpec(memory_space=pltpu.VMEM)
     mean, covs = pl.pallas_call(
         functools.partial(filter_kernel, steps, count),

time: 61.4 us -> 36 us (0.59)
  blocking collectives: 36.3 us -> 0 us
  Pallas kernels: 22.3 us -> 31.7 us
  other arithmetic: 0.01 us -> 1.88 us
    all_gather x1 -> x0, blocking collectives: 36.3 us -> none  [local(): data = lax.all_gather(packed, ('chain', 'leaf'), axis=0, tiled=True)]
    pallas_call x0 -> x1, Pallas kernels: none -> 9.33 us  [gathered(): pl.pallas_call(functools.partial(gather_kernel, chains, leaves), out_shap...]
    concatenate x0 -> x1, other arithmetic: none -> 1.22 us  [local(): jnp.concatenate([observations, observed.astype(jnp.float32), jnp.broadcas...]
    convert_element_type x1, other arithmetic: 0.01 us -> 0.66 us  [local(): observed.astype(jnp.float32)]
    unnamed x7 -> x4, local copies, waits for them, and re-layouts: 1.29 us -> 0.8 us
where the time goes in v1:
time: 36 us; the launch traced here: 35.7 us
  Pallas kernels  31.7 us (88%)
  other arithmetic  1.88 us (5%)
  between operations  1.35 us (4%)
  local copies, waits for them, and re-layouts  0.8 us (2%)
    pallas_call x1, Pallas kernels, local(): pl.pallas_call(functools.partial(filter_kernel, steps, count), out_shape=...  22.4 us
    pallas_call x1, Pallas kernels, gathered(): pl.pallas_call(functools.partial(gather_kernel, chains, leaves), out_shap...  9.33 us
    concatenate x1, other arithmetic, local(): jnp.concatenate([observations, observed.astype(jnp.float32), jnp.broadcas...  1.22 us
    unnamed x4, local copies, waits for them, and re-layouts  0.8 us

profile of v1, /device:TPU:31, one launch (start us, length us, event | category | flops | bytes accessed | tf_op | source)
XLA Modules:
  0.0 35.7 jit_solution(6156090073459009679)
XLA Ops:
  0.6 0.0 copy-start.1
  1.3 0.7 %convert_element_type.3 = f32[1,128]{1,0:T(1,128)S(1)} convert(s32[1,128]{1,0:T(1,128)} %param.5) | non-fusion elementwise | flops 128 | bytes 1024 | tf_op jit(solution)/shard_map/convert_element_type | solution.py:235
  2.0 1.2 %reshape_maximum_fusion.mine_ref = f32[1,384]{1,0:T(1,128)} fusion(f32[384]{0:T(512)S(1)} %pad.2.clone, f32[1,128]{1,0:T(1,128)S(1)} %convert_element_type.3, f32[1,128]{1,0:T(1,128)} %param.4), kind=kLoop, calls=%fused_computation | loop fusion | flops 768 | bytes 4096 | tf_op jit(solution)/shard_map/concatenate | solution.py:234
  3.2 9.3 %shard_map.59 = f32[8,4,1,384]{3,2,1,0:T(1,128)} custom-call(f32[1,384]{1,0:T(1,128)} %reshape_maximum_fusion.mine_ref), custom_call_target="tpu_custom_call" | custom-call | tf_op jit(solution)/shard_map/pallas_call | solution.py:218
  12.6 0.0 copy-done.1
  12.6 0.0 copy-start
  12.6 0.8 %copy-done = f32[8,4,1,384]{3,2,1,0:T(1,128)S(1)} copy-done((f32[8,4,1,384]{3,2,1,0:T(1,128)S(1)}, f32[8,4,1,384]{3,2,1,0:T(1,128)}, u32[]{:S(2)}) %copy-start) | copy-done | bytes 49176
  13.4 22.4 %shard_map.60 = (f32[1,1,256]{2,1,0:T(1,128)}, f32[1,256,256]{2,1,0:T(8,128)}) custom-call(s32[1]{0:T(128)} %bitcast.place_ref, f32[32,1,384]{2,1,0:T(1,128)S(1)} %bitcast.5, f32[128,128]{1,0:T(8,128)S(1)} %copy-done.1), custom_call_target="tpu_custom_call" | custom-call | tf_op jit(solution)/shard_map/pallas_call | solution.py:239
  (2 shorter events, 0.0 us)
Async XLA Ops:
  0.6 11.9 %copy-start.1 = (f32[128,128]{1,0:T(8,128)S(1)}, f32[128,128]{1,0:T(8,128)}, u32[]{:S(2)}) copy-start(f32[128,128]{1,0:T(8,128)} %cov_ref.1) | copy-start | bytes 196612
  12.6 0.8 %copy-start = (f32[8,4,1,384]{3,2,1,0:T(1,128)S(1)}, f32[8,4,1,384]{3,2,1,0:T(1,128)}, u32[]{:S(2)}) copy-start(f32[8,4,1,384]{3,2,1,0:T(1,128)} %shard_map.59) | copy-start | bytes 147460

commit v2 on v1

--- a/solution.py
+++ b/solution.py
@@ -48,13 +48,14 @@
 
 
 def filter_kernel(steps, count, place_ref, data_ref, cov_ref, mean_ref, out_ref,
-                  coef, state, pred, left, power):
+                  coef, state, pred, left, power, woven):
     sites = cov_ref.shape[0]
     dim = 2 * sites
     f32 = jnp.float32
     rows = lax.broadcasted_iota(jnp.int32, (sites, sites), 0)
     cols = lax.broadcasted_iota(jnp.int32, (sites, sites), 1)
     eye = (rows == cols).astype(f32)
+    apart = (rows != cols).astype(f32).astype(jnp.bfloat16)
 
     for k in range(steps):
         for part, plane in ((0, 8), (1, 7), (2, 0)):
@@ -103,27 +104,25 @@
 
         diag = 1.0 + weight * jnp.sum(ppp * eye, axis=0, keepdims=True)
         scale = weight / diag
-        r = (eye - 1.0) * ppp * scale
         y = jnp.concatenate([ppp * scale, pvp * scale, (pmp - obs) * scale], axis=0)
-        rh, rl = split(r)
         yh, yl = split(y)
+        rh, rl = yh[:sites] * apart, yl[:sites] * apart
         r2 = fast(rh, rh)
         right = jnp.concatenate(
             [jnp.concatenate([rh, rl], axis=1)] * 2, axis=0)
         both = fast(jnp.concatenate([yh, yl], axis=1), right)
-        y = y + (both[:, :sites] + both[:, sites:])
+        y = y - (both[:, :sites] + both[:, sites:])
         trace = jnp.sum(r2 * eye)
         r2h = r2.astype(jnp.bfloat16)
-        yh = y.astype(jnp.bfloat16)
         ph, pl_ = split(pred[:sites, :])
+        yh, yl = split(y)
+        z = fast(r2h, ph)
         u = fast(yh, r2h)
-        z = fast(r2h, ph)
-        y = y + u
-        yh, yl = split(y)
-        last = fast(
-            jnp.concatenate([yh, yl, yh, u.astype(jnp.bfloat16)], axis=1),
-            jnp.concatenate([ph, ph, pl_, z.astype(jnp.bfloat16)], axis=0))
-        state[...] = pred[...] - last
+        main = fast(
+            jnp.concatenate([yh, yl, yh], axis=1),
+            jnp.concatenate([ph, ph, pl_], axis=0))
+        rest = fast(u.astype(jnp.bfloat16), (pred[:sites, :] + z).astype(jnp.bfloat16))
+        state[...] = (pred[...] - main) - rest
 
         @pl.when(jnp.logical_not(trace < SMALL))
         def _():
@@ -151,11 +150,17 @@
             source = lax.broadcasted_iota(jnp.int32, (dim, dim), 0)
             target = lax.broadcasted_iota(jnp.int32, (dim, dim), 1)
             move = (source == (target % 2) * sites + target // 2).astype(f32)
-            wide = exact(state[...], move)
-            source = lax.broadcasted_iota(jnp.int32, (dim, dim), 1)
-            target = lax.broadcasted_iota(jnp.int32, (dim, dim), 0)
-            back = (source == (target % 2) * sites + target // 2).astype(f32)
-            out_ref[pl.ds(k - start, 1)] = exact(back, wide[:dim])[None]
+            high, low = split(state[...])
+            tail = ((state[...] - high.astype(f32)) - low.astype(f32)).astype(jnp.bfloat16)
+            move = move.astype(jnp.bfloat16)
+            wide = fast(
+                jnp.concatenate([high, low, tail], axis=1),
+                jnp.concatenate([move, move, move], axis=0))
+            for part in range(2):
+                half = pl.ds(part * sites, sites)
+                woven[pl.ds(0, sites, stride=2), :] = wide[:sites, part * sites:(part + 1) * sites]
+                woven[pl.ds(1, sites, stride=2), :] = wide[sites:dim, part * sites:(part + 1) * sites]
+                out_ref[pl.ds(k - start, 1), :, half] = woven[...][None]
             mean_ref[pl.ds(k - start, 1)] = wide[dim:dim + 1][None]
 
         return 0
@@ -163,7 +168,7 @@
     lax.fori_loop(0, start + count, step, 0)
 
 
-def gather_kernel(chains, leaves, mine_ref, all_ref, own_sem, leaf_send, leaf_recv, chain_send, chain_recv):
+def gather_kernel(chains, leaves, obs_ref, seen_ref, gap_ref, all_ref, mine_ref, own_sem, leaf_send, leaf_recv, chain_send, chain_recv):
     leaf = lax.axis_index("leaf")
     chain = lax.axis_index("chain")
     barrier = pltpu.get_barrier_semaphore()
@@ -173,6 +178,11 @@
     for turn in range(1, leaves):
         there = lax.rem(leaf + turn, leaves)
         pl.semaphore_signal(barrier, inc=1, device_id={"leaf": there}, device_id_type=pl.DeviceIdType.MESH)
+    count, sites = obs_ref.shape
+    mine_ref[:, :sites] = obs_ref[...]
+    mine_ref[:, sites:2 * sites] = seen_ref[...].astype(jnp.float32)
+    for i in range(count):
+        mine_ref[i:i + 1, 2 * sites:] = jnp.full((1, sites), gap_ref[i], jnp.float32)
     own = pltpu.make_async_copy(mine_ref, all_ref.at[chain, leaf], own_sem)
     own.start()
     pl.semaphore_wait(barrier, chains + leaves - 2)
@@ -210,33 +220,30 @@
         copy.wait_send()
 
 
-def gathered(packed):
+def gathered(observations, observed, gaps):
     leaves = lax.axis_size("leaf")
     chains = lax.axis_size("chain")
+    count, sites = observations.shape
     vmem = pl.BlockSpec(memory_space=pltpu.VMEM)
     dma = pltpu.SemaphoreType.DMA
     return pl.pallas_call(
         functools.partial(gather_kernel, chains, leaves),
-        out_shape=jax.ShapeDtypeStruct((chains, leaves) + packed.shape, packed.dtype),
-        in_specs=[vmem],
+        out_shape=jax.ShapeDtypeStruct((chains, leaves, count, 3 * sites), jnp.float32),
+        in_specs=[vmem, vmem, pl.BlockSpec(memory_space=pltpu.SMEM)],
         out_specs=vmem,
-        scratch_shapes=[dma, dma((leaves - 1,)), dma((leaves - 1,)), dma((chains - 1,)), dma((chains - 1,))],
+        scratch_shapes=[
+            pltpu.VMEM((count, 3 * sites), jnp.float32),
+            dma, dma((leaves - 1,)), dma((leaves - 1,)), dma((chains - 1,)), dma((chains - 1,)),
+        ],
         compiler_params=pltpu.CompilerParams(collective_id=0, has_side_effects=True),
-    )(packed)
-
-
-def local(observations, observed, gaps, site_cov):
-    count, sites = observations.shape
+    )(observations, observed, gaps)
+
+
+def run_filter(place, data, site_cov, steps, count):
+    sites = site_cov.shape[0]
     dim = 2 * sites
-    devices = lax.axis_size("leaf") * lax.axis_size("chain")
-    place = lax.axis_index("chain") * lax.axis_size("leaf") + lax.axis_index("leaf")
-    steps = count * devices
-    packed = jnp.concatenate(
-        [observations, observed.astype(jnp.float32),
-         jnp.broadcast_to(gaps[:, None], (count, sites))], axis=1)
-    data = gathered(packed).reshape(devices, count, 3 * sites)
     vmem = pl.BlockSpec(memory_space=pltpu.VMEM)
-    mean, covs = pl.pallas_call(
+    return pl.pallas_call(
         functools.partial(filter_kernel, steps, count),
         out_shape=(
             jax.ShapeDtypeStruct((count, 1, dim), jnp.float32),
@@ -250,9 +257,20 @@
             pltpu.VMEM((dim + PAD, dim), jnp.float32),
             pltpu.VMEM((dim + PAD, sites), jnp.float32),
             pltpu.VMEM((sites, sites), jnp.float32),
+            pltpu.VMEM((dim, sites), jnp.float32),
         ],
         compiler_params=pltpu.CompilerParams(vmem_limit_bytes=32 * 1024 * 1024),
-    )(jnp.reshape(place, (1,)).astype(jnp.int32), data, site_cov)
+    )(place, data, site_cov)
+
+
+def local(observations, observed, gaps, site_cov):
+    count, sites = observations.shape
+    dim = 2 * sites
+    devices = lax.axis_size("leaf") * lax.axis_size("chain")
+    place = lax.axis_index("chain") * lax.axis_size("leaf") + lax.axis_index("leaf")
+    steps = count * devices
+    data = gathered(observations, observed, gaps).reshape(devices, count, 3 * sites)
+    mean, covs = run_filter(jnp.reshape(place, (1,)).astype(jnp.int32), data, site_cov, steps, count)
     return mean.reshape(count, dim), covs
 
 

time: 36 us -> 30.6 us (0.85)
  Pallas kernels: 31.7 us -> 28.2 us
  other arithmetic: 1.88 us -> 0 us
    pallas_call x1, Pallas kernels: 22.4 us -> 18.9 us  [run_filter(): pl.pallas_call(functools.partial(filter_kernel, steps, count), out_shape=...]
    concatenate x1 -> x0, other arithmetic: 1.22 us -> none  [local(): jnp.concatenate([observations, observed.astype(jnp.float32), jnp.broadcas...]
    convert_element_type x1 -> x0, other arithmetic: 0.66 us -> none  [local(): observed.astype(jnp.float32)]
where the time goes in v2:
time: 30.6 us; the launch traced here: 30.4 us
  Pallas kernels  28.2 us (92%)
  between operations  1.35 us (4%)
  local copies, waits for them, and re-layouts  0.8 us (3%)
    pallas_call x1, Pallas kernels, run_filter(): pl.pallas_call(functools.partial(filter_kernel, steps, count), out_shape=...  18.9 us
    pallas_call x1, Pallas kernels, gathered(): pl.pallas_call(functools.partial(gather_kernel, chains, leaves), out_shap...  9.34 us
    unnamed x4, local copies, waits for them, and re-layouts  0.8 us

profile of v2, /device:TPU:31, one launch (start us, length us, event | category | flops | bytes accessed | tf_op | source)
XLA Modules:
  0.0 30.4 jit_solution(7647247678661828134)
XLA Ops:
  0.6 0.0 copy-start.1
  1.3 9.3 %shard_map.59 = f32[8,4,1,384]{3,2,1,0:T(1,128)} custom-call(f32[1,128]{1,0:T(1,128)} %obs_ref.1, s32[1,128]{1,0:T(1,128)} %seen_ref.1, f32[1]{0:T(128)S(6)} %copy.6.gap_ref), custom_call_target="tpu_custom_call" | custom-call | tf_op jit(solution)/shard_map/pallas_call | solution.py:229
  10.7 0.0 copy-done.1
  10.7 0.0 copy-start
  10.7 0.8 %copy-done = f32[8,4,1,384]{3,2,1,0:T(1,128)S(1)} copy-done((f32[8,4,1,384]{3,2,1,0:T(1,128)S(1)}, f32[8,4,1,384]{3,2,1,0:T(1,128)}, u32[]{:S(2)}) %copy-start) | copy-done | bytes 49176
  11.5 18.9 %shard_map.60 = (f32[1,1,256]{2,1,0:T(1,128)}, f32[1,256,256]{2,1,0:T(8,128)}) custom-call(s32[1]{0:T(128)} %bitcast.place_ref, f32[32,1,384]{2,1,0:T(1,128)S(1)} %bitcast.3, f32[128,128]{1,0:T(8,128)S(1)} %copy-done.1), custom_call_target="tpu_custom_call" | custom-call | tf_op jit(solution)/shard_map/pallas_call | solution.py:246
Async XLA Ops:
  0.6 10.0 %copy-start.1 = (f32[128,128]{1,0:T(8,128)S(1)}, f32[128,128]{1,0:T(8,128)}, u32[]{:S(2)}) copy-start(f32[128,128]{1,0:T(8,128)} %cov_ref.1) | copy-start | bytes 196612
  10.7 0.8 %copy-start = (f32[8,4,1,384]{3,2,1,0:T(1,128)S(1)}, f32[8,4,1,384]{3,2,1,0:T(1,128)}, u32[]{:S(2)}) copy-start(f32[8,4,1,384]{3,2,1,0:T(1,128)} %shard_map.59) | copy-start | bytes 147460

commit v3 on v2

--- a/solution.py
+++ b/solution.py
@@ -168,16 +168,21 @@
     lax.fori_loop(0, start + count, step, 0)
 
 
-def gather_kernel(chains, leaves, obs_ref, seen_ref, gap_ref, all_ref, mine_ref, own_sem, leaf_send, leaf_recv, chain_send, chain_recv):
+def gather_kernel(chains, leaves, obs_ref, seen_ref, gap_ref, all_ref, mine_ref, own_sem, send_sem, recv_sem):
+    total = chains * leaves
+    chain = lax.axis_index("chain")
     leaf = lax.axis_index("leaf")
-    chain = lax.axis_index("chain")
+    me = chain * leaves + leaf
     barrier = pltpu.get_barrier_semaphore()
-    for turn in range(1, chains):
-        there = lax.rem(chain + turn, chains)
-        pl.semaphore_signal(barrier, inc=1, device_id={"chain": there}, device_id_type=pl.DeviceIdType.MESH)
-    for turn in range(1, leaves):
-        there = lax.rem(leaf + turn, leaves)
-        pl.semaphore_signal(barrier, inc=1, device_id={"leaf": there}, device_id_type=pl.DeviceIdType.MESH)
+
+    def device(there):
+        return {"chain": there // leaves, "leaf": lax.rem(there, leaves)}
+
+    for turn in range(total - 1, 0, -1):
+        @pl.when(me >= turn)
+        def _():
+            pl.semaphore_signal(barrier, inc=1, device_id=device(me - turn), device_id_type=pl.DeviceIdType.MESH)
+
     count, sites = obs_ref.shape
     mine_ref[:, :sites] = obs_ref[...]
     mine_ref[:, sites:2 * sites] = seen_ref[...].astype(jnp.float32)
@@ -185,39 +190,33 @@
         mine_ref[i:i + 1, 2 * sites:] = jnp.full((1, sites), gap_ref[i], jnp.float32)
     own = pltpu.make_async_copy(mine_ref, all_ref.at[chain, leaf], own_sem)
     own.start()
-    pl.semaphore_wait(barrier, chains + leaves - 2)
-
-    sends = []
-    for turn in range(1, leaves):
-        copy = pltpu.make_async_remote_copy(
+    @pl.when(me < total - 1)
+    def _():
+        pl.semaphore_wait(barrier, total - 1 - me)
+
+    def sent(turn):
+        return pltpu.make_async_remote_copy(
             src_ref=mine_ref,
             dst_ref=all_ref.at[chain, leaf],
-            send_sem=leaf_send.at[turn - 1],
-            recv_sem=leaf_recv.at[turn - 1],
-            device_id={"leaf": lax.rem(leaf + turn, leaves)},
+            send_sem=send_sem.at[turn - 1],
+            recv_sem=recv_sem.at[turn - 1],
+            device_id=device(lax.rem(me + turn, total)),
             device_id_type=pl.DeviceIdType.MESH,
         )
-        copy.start()
-        sends.append(copy)
+
+    for turn in range(total - 1, 0, -1):
+        @pl.when(me + turn < total)
+        def _():
+            sent(turn).start()
     own.wait()
-    for copy in sends:
-        copy.wait_recv()
-    later = []
-    for turn in range(chains - 1, 0, -1):
-        copy = pltpu.make_async_remote_copy(
-            src_ref=all_ref.at[chain],
-            dst_ref=all_ref.at[chain],
-            send_sem=chain_send.at[turn - 1],
-            recv_sem=chain_recv.at[turn - 1],
-            device_id={"chain": lax.rem(chain + turn, chains)},
-            device_id_type=pl.DeviceIdType.MESH,
-        )
-        copy.start()
-        later.append(copy)
-    for copy in later:
-        copy.wait_recv()
-    for copy in sends + later:
-        copy.wait_send()
+    for turn in range(total - 1, 0, -1):
+        @pl.when(me >= turn)
+        def _():
+            sent(turn).wait_recv()
+
+        @pl.when(me + turn < total)
+        def _():
+            sent(turn).wait_send()
 
 
 def gathered(observations, observed, gaps):
@@ -233,7 +232,7 @@
         out_specs=vmem,
         scratch_shapes=[
             pltpu.VMEM((count, 3 * sites), jnp.float32),
-            dma, dma((leaves - 1,)), dma((leaves - 1,)), dma((chains - 1,)), dma((chains - 1,)),
+            dma, dma((chains * leaves - 1,)), dma((chains * leaves - 1,)),
         ],
         compiler_params=pltpu.CompilerParams(collective_id=0, has_side_effects=True),
     )(observations, observed, gaps)

time: 30.6 us -> 30.4 us (level)
  no operation moved by 1% of the time
where the time goes in v3:
time: 30.4 us; the launch traced here: 30.2 us
  Pallas kernels  28.1 us (92%)
  between operations  1.35 us (4%)
  local copies, waits for them, and re-layouts  0.8 us (3%)
    pallas_call x1, Pallas kernels, run_filter(): pl.pallas_call(functools.partial(filter_kernel, steps, count), out_shape=...  18.9 us
    pallas_call x1, Pallas kernels, gathered(): pl.pallas_call(functools.partial(gather_kernel, chains, leaves), out_shap...  9.15 us
    unnamed x4, local copies, waits for them, and re-layouts  0.8 us

profile of v3, /device:TPU:31, one launch (start us, length us, event | category | flops | bytes accessed | tf_op | source)
XLA Modules:
  0.0 30.2 jit_solution(11517707009248188677)
XLA Ops:
  0.6 0.0 copy-start.1
  1.3 9.1 %shard_map.59 = f32[8,4,1,384]{3,2,1,0:T(1,128)} custom-call(f32[1,128]{1,0:T(1,128)} %obs_ref.1, s32[1,128]{1,0:T(1,128)} %seen_ref.1, f32[1]{0:T(128)S(6)} %copy.6.gap_ref), custom_call_target="tpu_custom_call" | custom-call | tf_op jit(solution)/shard_map/pallas_call | solution.py:228
  10.5 0.0 copy-done.1
  10.5 0.0 copy-start
  10.5 0.8 %copy-done = f32[8,4,1,384]{3,2,1,0:T(1,128)S(1)} copy-done((f32[8,4,1,384]{3,2,1,0:T(1,128)S(1)}, f32[8,4,1,384]{3,2,1,0:T(1,128)}, u32[]{:S(2)}) %copy-start) | copy-done | bytes 49176
  11.3 18.9 %shard_map.60 = (f32[1,1,256]{2,1,0:T(1,128)}, f32[1,256,256]{2,1,0:T(8,128)}) custom-call(s32[1]{0:T(128)} %bitcast.place_ref, f32[32,1,384]{2,1,0:T(1,128)S(1)} %bitcast.3, f32[128,128]{1,0:T(8,128)S(1)} %copy-done.1), custom_call_target="tpu_custom_call" | custom-call | tf_op jit(solution)/shard_map/pallas_call | solution.py:245
Async XLA Ops:
  0.6 9.9 %copy-start.1 = (f32[128,128]{1,0:T(8,128)S(1)}, f32[128,128]{1,0:T(8,128)}, u32[]{:S(2)}) copy-start(f32[128,128]{1,0:T(8,128)} %cov_ref.1) | copy-start | bytes 196612
  10.5 0.8 %copy-start = (f32[8,4,1,384]{3,2,1,0:T(1,128)S(1)}, f32[8,4,1,384]{3,2,1,0:T(1,128)}, u32[]{:S(2)}) copy-start(f32[8,4,1,384]{3,2,1,0:T(1,128)} %shard_map.59) | copy-start | bytes 147460
